TPU v7x, 256 devices: a whole 4x4x8 slice. The times are simulated.
256 devices in a mesh: rows: 16 (over x, y), cols: 16 (over z, core).
Axes of the slice: x: 4, y: 4, z: 8, core: 2. Of those that a mesh axis runs over, the one named last changes fastest.
Arguments:
- power: float32 [2, 4, 2048, 2048], P(None, None, 'rows', 'cols'), may hold values from -6 to 6
- material: int32 [4, 2048, 2048], P(None, 'rows', 'cols'), may hold values from 0 to 7
- cond_table: float32 [4, 8], replicated, may hold values from 0.5 to 8
- tier_table: int32 [4], replicated, may hold values from 0 to 3
- coarse_slot: int32 [256], replicated, may hold values from 0 to 255, each once
- coarse_inverse: float32 [16, 16, 16], replicated, as said below
Outputs:
- solution: float32 [2, 4, 2048, 2048], P(None, None, 'rows', 'cols')
- residual: float32 [2, 4, 2048, 2048], P(None, None, 'rows', 'cols')
- precond: float32 [2, 4, 2048, 2048], P(None, None, 'rows', 'cols')
Inputs may be any that keep to these rules, and one draw needn't show every extreme that they name: `coarse_slot`: each value once. `coarse_inverse`: symmetric within each owner.
All inputs are finite; a program needn't handle non-finite values.
Results may differ from a plain program's by a relative error of at most 0.0003.
Values sent between devices are 32-bit elements; how exact they have to be, the bound alone decides.
No kernel may reach another device: no remote copies, remote signals or barrier semaphores. Data moves between devices by JAX's collectives and lax.ppermute only.
A program may use at most 64 MiB of HBM per device.

v0:
```python
import math
import jax
import jax.numpy as jnp
from jax import lax
from jax.sharding import PartitionSpec as P

SUB = 128
TIERS = 4
ITERS = 2
SHIFT_C = 0.5
VERT_C = 2.0
SINK_C = 0.05
HIGH = lax.Precision.HIGHEST


def with_halo(cells, sides, width):
    for axis, dim in sides:
        count = lax.axis_size(axis)
        ends = count - 1
        head = lax.slice_in_dim(cells, 0, width, axis=dim)
        tail = lax.slice_in_dim(cells, cells.shape[dim] - width, cells.shape[dim], axis=dim)
        cells = jnp.concatenate(
            [
                lax.ppermute(tail, axis, [(i, (i + 1) % count) for i in range(ends)]),
                cells,
                lax.ppermute(head, axis, [((i + 1) % count, i) for i in range(ends)]),
            ],
            axis=dim,
        )
    return cells


def sine_basis(length):
    counting = jnp.arange(1, length + 1).astype(jnp.float32)
    step_angle = math.pi / (length + 1)
    basis = math.sqrt(2.0 / (length + 1)) * jnp.sin(
        step_angle * counting[:, None] * counting[None, :]
    )
    eigen_values = 2.0 - 2.0 * jnp.cos(step_angle * counting)
    return (basis, eigen_values)


def conductivity(material, cond_table, tier_table):
    tables = cond_table.shape[0]
    picker = (tier_table[:, None] == jnp.arange(tables, dtype=jnp.int32)[None, :]).astype(
        jnp.float32
    )
    tier_rows = jnp.dot(picker, cond_table, precision=HIGH)
    cond = jnp.zeros(material.shape, jnp.float32)
    for number in range(cond_table.shape[1]):
        cond = cond + jnp.where(material == number, tier_rows[:, number][:, None, None], 0.0)
    return (cond, jnp.mean(tier_rows, axis=1))


def coefficients(cond, padded):
    north = 0.5 * (cond + padded[:, :-2, 1:-1])
    south = 0.5 * (cond + padded[:, 2:, 1:-1])
    west = 0.5 * (cond + padded[:, 1:-1, :-2])
    east = 0.5 * (cond + padded[:, 1:-1, 2:])
    upward = VERT_C * 0.5 * (cond[:-1] + cond[1:])
    sink = jnp.concatenate([SINK_C * cond[:1], jnp.zeros_like(cond[1:])], 0)
    return (north, south, west, east, upward, sink)


def operate(temps, padded, coefs):
    north, south, west, east, upward, sink = coefs
    lateral = north * (temps - padded[:, :, :-2, 1:-1]) + south * (temps - padded[:, :, 2:, 1:-1])
    lateral = (
        lateral + west * (temps - padded[:, :, 1:-1, :-2]) + east * (temps - padded[:, :, 1:-1, 2:])
    )
    flux = upward * (temps[:, :-1] - temps[:, 1:])
    zeros_tier = jnp.zeros_like(temps[:, :1])
    vertical = jnp.concatenate([flux, zeros_tier], 1) - jnp.concatenate([zeros_tier, flux], 1)
    return lateral + vertical + sink * temps


def block_solve(temps, basis, denominator):
    shape = temps.shape
    length = basis.shape[0]
    blocks = temps.reshape(
        shape[0], shape[1], shape[2] // length, length, shape[3] // length, length
    )
    spectral = jnp.einsum("ia,vtxayb->vtxiyb", basis, blocks, precision=HIGH)
    spectral = jnp.einsum("vtxiyb,bj->vtxiyj", spectral, basis, precision=HIGH)
    spectral = spectral / denominator[None, :, None, :, None, :]
    result = jnp.einsum("ia,vtxayb->vtxiyb", basis, spectral, precision=HIGH)
    result = jnp.einsum("vtxiyb,bj->vtxiyj", result, basis, precision=HIGH)
    return result.reshape(shape)


def pad_rim(values):
    return with_halo(values, (("rows", 2), ("cols", 3)), 1)


def inner_local(left_arr, right_arr):
    return jnp.sum(left_arr * right_arr, axis=(1, 2, 3))


def shards(power, material, cond_table, tier_table, coarse_slot, coarse_inverse):
    cond, mean_cond = conductivity(material, cond_table, tier_table)
    coefs = coefficients(cond, pad_rim(cond[None])[0])
    basis, eigen_values = sine_basis(SUB)
    denominator = mean_cond[:, None, None] * (
        eigen_values[:, None] + eigen_values[None, :] + SHIFT_C
    )
    half = SUB // 2
    scale = 1.0 / math.sqrt(SUB * SUB * TIERS)
    tile = power.shape[2]
    blocks_side = tile // SUB
    total = coarse_slot.shape[0]
    row_index = lax.axis_index("rows")
    col_index = lax.axis_index("cols")
    row_ids = row_index * blocks_side + jnp.arange(blocks_side, dtype=jnp.int32)
    col_ids = col_index * blocks_side + jnp.arange(blocks_side, dtype=jnp.int32)
    global_ids = (
        row_ids[:, None] * (lax.axis_size("cols") * blocks_side) + col_ids[None, :]
    ).reshape(-1)
    columns = jnp.arange(total, dtype=jnp.int32)
    local_slot = jnp.sum(
        jnp.where(global_ids[:, None] == columns[None, :], coarse_slot[None, :], 0), axis=1
    )
    placer = (local_slot[:, None] == columns[None, :]).astype(jnp.float32)
    owners = coarse_inverse.shape[0]
    own_count = coarse_inverse.shape[1]

    def precondition(resid):
        variants = resid.shape[0]
        aligned = block_solve(resid, basis, denominator)
        extended = with_halo(resid, (("rows", 2), ("cols", 3)), half)
        positions = jnp.arange(tile + SUB, dtype=jnp.int32)
        mask_rows = jnp.where((positions < SUB) & (row_index == 0), 0.0, 1.0)
        mask_cols = jnp.where((positions < SUB) & (col_index == 0), 0.0, 1.0)
        solved_ext = (
            block_solve(extended, basis, denominator) * mask_rows[:, None] * mask_cols[None, :]
        )
        offset = solved_ext[:, :, half : half + tile, half : half + tile]
        sums = (
            resid.reshape(variants, TIERS, blocks_side, SUB, blocks_side, SUB).sum(axis=(1, 3, 5))
            * scale
        )
        ordered = jnp.einsum(
            "sc,vs->cv", placer, sums.reshape(variants, blocks_side * blocks_side), precision=HIGH
        )
        stacked = ordered.reshape(owners, own_count, variants)
        owned = lax.psum_scatter(stacked, "cols", scatter_dimension=0, tiled=True)
        owned = lax.psum(owned, "rows")
        mine = lax.dynamic_slice_in_dim(coarse_inverse, col_index, 1, 0)
        own_sol = jnp.einsum("okj,ojv->okv", mine, owned, precision=HIGH)
        every_sol = lax.all_gather(own_sol, "cols", axis=0, tiled=True)
        picked = jnp.einsum("sc,cv->vs", placer, every_sol.reshape(total, variants), precision=HIGH)
        picked = picked.reshape(variants, 1, blocks_side, 1, blocks_side, 1)
        coarse = jnp.broadcast_to(picked, (variants, TIERS, blocks_side, SUB, blocks_side, SUB))
        return aligned + offset + coarse.reshape(resid.shape) * scale

    solution = jnp.zeros_like(power)
    residual = power
    precond = precondition(residual)
    direction = precond

    def rz_sum(left_arr, right_arr):
        return lax.psum(inner_local(left_arr, right_arr), ("rows", "cols"))

    rz_now = rz_sum(residual, precond)
    for number in range(ITERS):
        image = operate(direction, pad_rim(direction), coefs)
        alpha = rz_now / lax.psum(inner_local(direction, image), ("rows", "cols"))
        solution = solution + alpha[:, None, None, None] * direction
        residual = residual - alpha[:, None, None, None] * image
        precond = precondition(residual)
        rz_next = rz_sum(residual, precond)
        direction = precond + (rz_next / rz_now)[:, None, None, None] * direction
        rz_now = rz_next
    return (solution, residual, precond)


def solution(mesh):
    in_specs = (P(None, None, "rows", "cols"), P(None, "rows", "cols"), P(), P(), P(), P())
    out_specs = (
        P(None, None, "rows", "cols"),
        P(None, None, "rows", "cols"),
        P(None, None, "rows", "cols"),
    )
    return jax.shard_map(shards, mesh=mesh, in_specs=in_specs, out_specs=out_specs, check_vma=False)
```

profile of v0, /device:TPU:1, one launch (start us, length us, event | category | flops | bytes accessed | tf_op | source)
XLA Modules:
  0.0 762.5 jit_solution(1685460788034805416)
XLA Ops:
  4.4 4.7 collective-permute-start
  12.0 4.0 collective-permute-start.4
  18.7 48.1 %all-reduce.5 = f32[16,16,2]{1,2,0:T(2,128)S(1)} all-reduce(f32[16,16,2]{1,2,0:T(2,128)S(1)} %broadcast_multiply_fusion.3), channel_id=5, replica_groups=mesh['rows'=16,'cols'=16] {'cols'}, use_global_device_ids=true, to_apply=%region_3.4.clone | all-reduce | flops 512 | bytes 4096
  68.2 32.1 %psum.49 = f32[16,2]{0,1:T(2,128)S(1)} all-reduce(f32[16,2]{0,1:T(2,128)S(1)} %dynamic-slice_bitcast_fusion.2), channel_id=1, replica_groups=mesh['rows'=16,'cols'=16] {'rows'}, use_global_device_ids=true, to_apply=%region_4.5 | all-reduce | flops 32 | bytes 256 | tf_op jit(solution)/shard_map/psum | solution.py:146
  100.5 24.5 %all-gather.3 = f32[16,16,2]{1,2,0:T(2,128)S(1)} all-gather(f32[1,16,2]{1,2,0:T(2,128)S(1)} %convolution_bitcast_fusion.8), channel_id=2, replica_groups=mesh['rows'=16,'cols'=16] {'cols'}, dimensions={0}, use_global_device_ids=true | all-gather | bytes 2176 | tf_op jit(solution)/shard_map/all_gather | solution.py:149
  139.8 3.6 collective-permute-start.6
  154.4 3.6 fusion.10
  158.0 3.8 fusion.22
  161.7 4.1 fusion.8
  174.1 4.0 collective-permute-start.8
  185.6 5.0 collective-permute-start.10
  195.7 78.5 %all-reduce.8 = (f32[2]{0:T(128)S(1)}, f32[2]{0:T(128)S(1)}) all-reduce(f32[2]{0:T(128)S(1)} %get-tuple-element.4, f32[2]{0:T(128)S(1)} %get-tuple-element.3), channel_id=1, replica_groups=mesh['rows'=16,'cols'=16] {'rows','cols'}, use_global_device_ids=true, to_apply=%region_6.7 | all-reduce | flops 4 | bytes 32 | tf_op jit(solution)/shard_map/psum | solution.py:161
  275.4 44.4 %all-reduce.6 = f32[16,16,2]{1,2,0:T(2,128)S(1)} all-reduce(f32[16,16,2]{1,2,0:T(2,128)S(1)} %broadcast_multiply_fusion.2), channel_id=6, replica_groups=mesh['rows'=16,'cols'=16] {'cols'}, use_global_device_ids=true, to_apply=%region_10.11.clone | all-reduce | flops 512 | bytes 4096
  320.5 29.8 %psum.52 = f32[16,2]{0,1:T(2,128)S(1)} all-reduce(f32[16,2]{0,1:T(2,128)S(1)} %dynamic-slice_bitcast_fusion.1), channel_id=1, replica_groups=mesh['rows'=16,'cols'=16] {'rows'}, use_global_device_ids=true, to_apply=%region_11.12 | all-reduce | flops 32 | bytes 256 | tf_op jit(solution)/shard_map/psum | solution.py:146
  351.6 4.0 collective-permute-start.12
  355.8 25.2 %all-gather.4 = f32[16,16,2]{1,2,0:T(2,128)S(1)} all-gather(f32[1,16,2]{1,2,0:T(2,128)S(1)} %convolution_bitcast_fusion.7), channel_id=3, replica_groups=mesh['rows'=16,'cols'=16] {'cols'}, dimensions={0}, use_global_device_ids=true | all-gather | bytes 2176 | tf_op jit(solution)/shard_map/all_gather | solution.py:149
  409.3 5.2 fusion.16
  418.1 3.8 fusion.20
  421.9 4.1 fusion.4
  429.0 3.9 reshape.324
  435.4 74.4 %psum.53 = f32[2]{0:T(128)S(1)} all-reduce(f32[2]{0:T(128)S(1)} %get-tuple-element.53), channel_id=1, replica_groups=mesh['rows'=16,'cols'=16] {'rows','cols'}, use_global_device_ids=true, to_apply=%region_13.14 | all-reduce | flops 2 | bytes 16 | tf_op jit(solution)/shard_map/psum | solution.py:161
  511.3 4.0 collective-permute-start.16
  518.8 3.7 collective-permute-start.19
  532.2 78.1 %psum.54 = f32[2]{0:T(128)S(1)} all-reduce(f32[2]{0:T(128)} %get-tuple-element.17), channel_id=1, replica_groups=mesh['rows'=16,'cols'=16] {'rows','cols'}, use_global_device_ids=true, to_apply=%region_15.16 | all-reduce | flops 2 | bytes 16 | tf_op jit(solution)/shard_map/psum | solution.py:166
  614.1 4.0 collective-permute-start.20
  618.2 44.4 %all-reduce.7 = f32[16,16,2]{1,2,0:T(2,128)S(1)} all-reduce(f32[16,16,2]{1,2,0:T(2,128)S(1)} %broadcast_multiply_fusion.1), channel_id=7, replica_groups=mesh['rows'=16,'cols'=16] {'cols'}, use_global_device_ids=true, to_apply=%region_17.18.clone | all-reduce | flops 512 | bytes 4096
  663.3 29.1 %psum.55 = f32[16,2]{0,1:T(2,128)S(1)} all-reduce(f32[16,2]{0,1:T(2,128)S(1)} %dynamic-slice_bitcast_fusion), channel_id=1, replica_groups=mesh['rows'=16,'cols'=16] {'rows'}, use_global_device_ids=true, to_apply=%region_18.19 | all-reduce | flops 32 | bytes 256 | tf_op jit(solution)/shard_map/psum | solution.py:146
  692.5 24.7 %all-gather.5 = f32[16,16,2]{1,2,0:T(2,128)S(1)} all-gather(f32[1,16,2]{1,2,0:T(2,128)S(1)} %convolution_bitcast_fusion.6), channel_id=4, replica_groups=mesh['rows'=16,'cols'=16] {'cols'}, dimensions={0}, use_global_device_ids=true | all-gather | bytes 2176 | tf_op jit(solution)/shard_map/all_gather | solution.py:149
  739.7 3.7 fusion.14
  743.4 3.6 fusion.2
  747.0 3.8 fusion.18
  750.8 3.9 fusion
  (259 shorter events, 146.5 us)
Async XLA Ops:
  0.6 99.7 %copy-start = (f32[16,16,16]{2,1,0:T(8,128)S(1)}, f32[16,16,16]{2,1,0:T(8,128)}, u32[]{:S(2)}) copy-start(f32[16,16,16]{2,1,0:T(8,128)} %param.11) | copy-start | bytes 49156
  3.1 127.2 %collective-permute-start.1 = (f32[2,4,64,128]{2,3,1,0:T(8,128)}, f32[2,4,64,128]{2,3,1,0:T(8,128)S(1)}, u32[]{:S(2)}, u32[]{:S(2)}) collective-permute-start(f32[2,4,64,128]{2,3,1,0:T(8,128)} %get-tuple-element.45), channel_id=1, source_target_pairs={{16,0},{32,16},{48,32},{64,48},{80,64},{96,80},{112,96},{128,112},... | collective-permute-start | bytes 786440 | tf_op jit(solution)/shard_map/ppermute | solution.py:26
  4.4 125.9 %collective-permute-start = (f32[2,4,64,128]{2,3,1,0:T(8,128)}, f32[2,4,64,128]{2,3,1,0:T(8,128)S(1)}, u32[]{:S(2)}, u32[]{:S(2)}) collective-permute-start(f32[2,4,64,128]{2,3,1,0:T(8,128)} %get-tuple-element.44), channel_id=1, source_target_pairs={{0,16},{16,32},{32,48},{48,64},{64,80},{80,96},{96,112},{112,128},... | collective-permute-start | bytes 786440 | tf_op jit(solution)/shard_map/ppermute | solution.py:24
  9.7 118.6 %copy-start.25 = (f32[4]{0:T(128)}, f32[4]{0:T(128)S(1)}, u32[]{:S(2)}) copy-start(f32[4]{0:T(128)S(1)} %get-tuple-element.5) | copy-start | bytes 52
  9.7 118.6 %copy-start.27 = (f32[4]{0:T(128)}, f32[4]{0:T(128)S(1)}, u32[]{:S(2)}) copy-start(f32[4]{0:T(128)S(1)} %get-tuple-element.6) | copy-start | bytes 52
  9.8 118.6 %copy-start.29 = (f32[4]{0:T(128)}, f32[4]{0:T(128)S(1)}, u32[]{:S(2)}) copy-start(f32[4]{0:T(128)S(1)} %get-tuple-element.7) | copy-start | bytes 52
  9.8 118.6 %copy-start.31 = (f32[4]{0:T(128)}, f32[4]{0:T(128)S(1)}, u32[]{:S(2)}) copy-start(f32[4]{0:T(128)S(1)} %get-tuple-element.8) | copy-start | bytes 52
  9.8 118.6 %copy-start.33 = (f32[4]{0:T(128)}, f32[4]{0:T(128)S(1)}, u32[]{:S(2)}) copy-start(f32[4]{0:T(128)S(1)} %get-tuple-element.9) | copy-start | bytes 52
  9.8 118.6 %copy-start.35 = (f32[4]{0:T(128)}, f32[4]{0:T(128)S(1)}, u32[]{:S(2)}) copy-start(f32[4]{0:T(128)S(1)} %get-tuple-element.10) | copy-start | bytes 52
  10.7 125.8 %collective-permute-start.5 = (f32[1,4,1,128]{3,2,1,0:T(1,128)}, f32[1,4,1,128]{3,2,1,0:T(1,128)S(1)}, u32[]{:S(2)}, u32[]{:S(2)}) collective-permute-start(f32[1,4,1,128]{3,2,1,0:T(1,128)} %get-tuple-element.49), channel_id=1, source_target_pairs={{16,0},{32,16},{48,32},{64,48},{80,64},{96,80},{112,96},{128,112},... | collective-permute-start | bytes 6152 | tf_op jit(solution)/shard_map/ppermute | solution.py:26
  12.0 124.5 %collective-permute-start.4 = (f32[1,4,1,128]{3,2,1,0:T(1,128)}, f32[1,4,1,128]{3,2,1,0:T(1,128)S(1)}, u32[]{:S(2)}, u32[]{:S(2)}) collective-permute-start(f32[1,4,1,128]{3,2,1,0:T(1,128)} %get-tuple-element.48), channel_id=1, source_target_pairs={{0,16},{16,32},{32,48},{48,64},{64,80},{80,96},{96,112},{112,128},... | collective-permute-start | bytes 6152 | tf_op jit(solution)/shard_map/ppermute | solution.py:24
  130.9 17.0 %collective-permute-start.3 = (f32[2,4,256,64]{2,3,1,0:T(8,128)S(1)}, f32[2,4,256,64]{2,3,1,0:T(8,128)S(1)}, u32[]{:S(2)}, u32[]{:S(2)}) collective-permute-start(f32[2,4,256,64]{2,3,1,0:T(8,128)S(1)} %get-tuple-element.27), channel_id=1, source_target_pairs={{1,0},{2,1},{3,2},{4,3},{5,4},{6,5},{7,6},{8,7},{9,8},{10,9},{11,1... | collective-permute-start | bytes 1572872 | tf_op jit(solution)/shard_map/ppermute | solution.py:26
  133.0 14.9 %collective-permute-start.2 = (f32[2,4,256,64]{2,3,1,0:T(8,128)S(1)}, f32[2,4,256,64]{2,3,1,0:T(8,128)S(1)}, u32[]{:S(2)}, u32[]{:S(2)}) collective-permute-start(f32[2,4,256,64]{2,3,1,0:T(8,128)S(1)} %get-tuple-element.26), channel_id=1, source_target_pairs={{0,1},{1,2},{2,3},{3,4},{4,5},{5,6},{6,7},{7,8},{8,9},{9,10},{10,1... | collective-permute-start | bytes 1572872 | tf_op jit(solution)/shard_map/ppermute | solution.py:24
  137.8 7.9 %collective-permute-start.7 = (f32[1,4,130,1]{3,2,1,0:T(8,128)S(1)}, f32[1,4,130,1]{3,2,1,0:T(8,128)S(1)}, u32[]{:S(2)}, u32[]{:S(2)}) collective-permute-start(f32[1,4,130,1]{3,2,1,0:T(8,128)S(1)} %get-tuple-element.47), channel_id=1, source_target_pairs={{1,0},{2,1},{3,2},{4,3},{5,4},{6,5},{7,6},{8,7},{9,8},{10,9},{11,1... | collective-permute-start | bytes 6248 | tf_op jit(solution)/shard_map/ppermute | solution.py:26
  139.8 7.1 collective-permute-start.6
  172.8 6.8 collective-permute-start.9
  174.1 5.5 collective-permute-start.8
  182.3 9.1 %collective-permute-start.11 = (f32[2,4,130,1]{2,1,3,0:T(4,128)S(1)}, f32[2,4,130,1]{2,1,3,0:T(4,128)S(1)}, u32[]{:S(2)}, u32[]{:S(2)}) collective-permute-start(f32[2,4,130,1]{2,1,3,0:T(4,128)S(1)} %copy.90), channel_id=1, source_target_pairs={{1,0},{2,1},{3,2},{4,3},{5,4},{6,5},{7,6},{8,7},{9,8},{10,9},{11,1... | collective-permute-start | bytes 12488 | tf_op jit(solution)/shard_map/ppermute | solution.py:26
  185.6 6.8 collective-permute-start.10
  350.3 32.7 %collective-permute-start.13 = (f32[2,4,64,128]{3,2,1,0:T(8,128)S(1)}, f32[2,4,64,128]{3,2,1,0:T(8,128)S(1)}, u32[]{:S(2)}, u32[]{:S(2)}) collective-permute-start(f32[2,4,64,128]{3,2,1,0:T(8,128)S(1)} %get-tuple-element.41), channel_id=1, source_target_pairs={{16,0},{32,16},{48,32},{64,48},{80,64},{96,80},{112,96},{128,112},... | collective-permute-start | bytes 786440 | tf_op jit(solution)/shard_map/ppermute | solution.py:26
  351.6 31.4 %collective-permute-start.12 = (f32[2,4,64,128]{3,2,1,0:T(8,128)S(1)}, f32[2,4,64,128]{3,2,1,0:T(8,128)S(1)}, u32[]{:S(2)}, u32[]{:S(2)}) collective-permute-start(f32[2,4,64,128]{3,2,1,0:T(8,128)S(1)} %get-tuple-element.40), channel_id=1, source_target_pairs={{0,16},{16,32},{32,48},{48,64},{64,80},{80,96},{96,112},{112,128},... | collective-permute-start | bytes 786440 | tf_op jit(solution)/shard_map/ppermute | solution.py:24
  386.8 10.8 %collective-permute-start.15 = (f32[2,4,256,64]{2,3,1,0:T(8,128)}, f32[2,4,256,64]{2,3,1,0:T(8,128)}, u32[]{:S(2)}, u32[]{:S(2)}) collective-permute-start(f32[2,4,256,64]{2,3,1,0:T(8,128)} %copy.97), channel_id=1, source_target_pairs={{1,0},{2,1},{3,2},{4,3},{5,4},{6,5},{7,6},{8,7},{9,8},{10,9},{11,1... | collective-permute-start | bytes 1572872 | tf_op jit(solution)/shard_map/ppermute | solution.py:26
  390.0 9.9 %collective-permute-start.14 = (f32[2,4,256,64]{2,3,1,0:T(8,128)}, f32[2,4,256,64]{2,3,1,0:T(8,128)}, u32[]{:S(2)}, u32[]{:S(2)}) collective-permute-start(f32[2,4,256,64]{2,3,1,0:T(8,128)} %copy.96), channel_id=1, source_target_pairs={{0,1},{1,2},{2,3},{3,4},{4,5},{5,6},{6,7},{7,8},{8,9},{9,10},{10,1... | collective-permute-start | bytes 1572872 | tf_op jit(solution)/shard_map/ppermute | solution.py:24
  510.0 5.3 collective-permute-start.17
  511.3 4.7 collective-permute-start.16
  518.8 8.5 %collective-permute-start.19 = (f32[2,4,130,1]{2,1,3,0:T(4,128)S(1)}, f32[2,4,130,1]{2,1,3,0:T(4,128)S(1)}, u32[]{:S(2)}, u32[]{:S(2)}) collective-permute-start(f32[2,4,130,1]{2,1,3,0:T(4,128)S(1)} %copy.108), channel_id=1, source_target_pairs={{1,0},{2,1},{3,2},{4,3},{5,4},{6,5},{7,6},{8,7},{9,8},{10,9},{11,1... | collective-permute-start | bytes 12488 | tf_op jit(solution)/shard_map/ppermute | solution.py:26
  523.9 4.5 collective-permute-start.18
  612.7 121.3 %copy-start.2 = (f32[2,4,128,128]{3,2,1,0:T(8,128)}, f32[2,4,128,128]{3,2,1,0:T(8,128)S(1)}, u32[]{:S(2)}) copy-start(f32[2,4,128,128]{3,2,1,0:T(8,128)S(1)} %get-tuple-element.16) | copy-start | bytes 1572868
  612.8 105.6 %collective-permute-start.21 = (f32[2,4,64,128]{3,2,1,0:T(8,128)S(1)}, f32[2,4,64,128]{3,2,1,0:T(8,128)S(1)}, u32[]{:S(2)}, u32[]{:S(2)}) collective-permute-start(f32[2,4,64,128]{3,2,1,0:T(8,128)S(1)} %get-tuple-element.37), channel_id=1, source_target_pairs={{16,0},{32,16},{48,32},{64,48},{80,64},{96,80},{112,96},{128,112},... | collective-permute-start | bytes 786440 | tf_op jit(solution)/shard_map/ppermute | solution.py:26
  614.1 104.4 %collective-permute-start.20 = (f32[2,4,64,128]{3,2,1,0:T(8,128)S(1)}, f32[2,4,64,128]{3,2,1,0:T(8,128)S(1)}, u32[]{:S(2)}, u32[]{:S(2)}) collective-permute-start(f32[2,4,64,128]{3,2,1,0:T(8,128)S(1)} %get-tuple-element.36), channel_id=1, source_target_pairs={{0,16},{16,32},{32,48},{48,64},{64,80},{80,96},{96,112},{112,128},... | collective-permute-start | bytes 786440 | tf_op jit(solution)/shard_map/ppermute | solution.py:24
  720.6 10.7 %collective-permute-start.23 = (f32[2,4,256,64]{2,3,1,0:T(8,128)}, f32[2,4,256,64]{2,3,1,0:T(8,128)S(1)}, u32[]{:S(2)}, u32[]{:S(2)}) collective-permute-start(f32[2,4,256,64]{2,3,1,0:T(8,128)} %copy.115), channel_id=1, source_target_pairs={{1,0},{2,1},{3,2},{4,3},{5,4},{6,5},{7,6},{8,7},{9,8},{10,9},{11,1... | collective-permute-start | bytes 1572872 | tf_op jit(solution)/shard_map/ppermute | solution.py:26
  723.0 9.6 %collective-permute-start.22 = (f32[2,4,256,64]{2,3,1,0:T(8,128)S(1)}, f32[2,4,256,64]{2,3,1,0:T(8,128)}, u32[]{:S(2)}, u32[]{:S(2)}) collective-permute-start(f32[2,4,256,64]{2,3,1,0:T(8,128)S(1)} %copy.114), channel_id=1, source_target_pairs={{0,1},{1,2},{2,3},{3,4},{4,5},{5,6},{6,7},{7,8},{8,9},{9,10},{10,1... | collective-permute-start | bytes 1572872 | tf_op jit(solution)/shard_map/ppermute | solution.py:24
  (45 other events, 519.4 us)
where the time goes:
time: 770 us; the launch traced here: 762 us
  blocking collectives  534 us (69%)
  matrix products  70.3 us (9%)
  starting transfers between devices  67.9 us (9%)
  local copies, waits for them, and re-layouts  58.5 us (8%)
  other arithmetic  24.1 us (3%)
    psum x2, blocking collectives, rz_sum(): return lax.psum(inner_local(left_arr, right_arr), ('rows', 'cols'))  153 us
    unnamed x3, blocking collectives  137 us
    psum x3, blocking collectives, precondition(): owned = lax.psum(owned, 'rows')  91.1 us
    psum x1, blocking collectives, shards(): alpha = rz_now / lax.psum(inner_local(direction, image), ('rows', 'cols'))  78.1 us
    all_gather x3, blocking collectives, precondition(): every_sol = lax.all_gather(own_sol, 'cols', axis=0, tiled=True)  74.4 us
    ppermute x12, starting transfers between devices, with_halo(): lax.ppermute(tail, axis, [(i, (i + 1) % count) for i in range(ends)])  46.4 us
    ppermute x12, starting transfers between devices, with_halo(): lax.ppermute(head, axis, [((i + 1) % count, i) for i in range(ends)])  21.5 us
    dot_general x6, matrix products, block_solve(): result = jnp.einsum('vtxiyb,bj->vtxiyj', result, basis, precision=HIGH)  20.4 us
  transfers between devices with their start and end apart: 24, of which 7 were waited for; matrix products, arithmetic and copies ran while one was open for 5% of the time, Pallas kernels for 0%

commit v1 on v0

--- a/solution.py
+++ b/solution.py
@@ -11,6 +11,11 @@
 VERT_C = 2.0
 SINK_C = 0.05
 HIGH = lax.Precision.HIGHEST
+
+
+def one_after_other(x, one, other):
+    partial = lax.psum(x, one)
+    return lax.psum(partial, other)
 
 
 def with_halo(cells, sides, width):
@@ -158,7 +163,7 @@
     direction = precond
 
     def rz_sum(left_arr, right_arr):
-        return lax.psum(inner_local(left_arr, right_arr), ("rows", "cols"))
+        return one_after_other(inner_local(left_arr, right_arr), "rows", "cols")
 
     rz_now = rz_sum(residual, precond)
     for number in range(ITERS):

time: 770 us -> 813 us (1.056)
  blocking collectives: 534 us -> 578 us
    psum x1 -> x2, blocking collectives: 78.1 us -> 156 us  [shards(): alpha = rz_now / lax.psum(inner_local(direction, image), ('rows', 'cols'))]
    psum x2 -> x4, blocking collectives: 153 us -> 119 us  [the longest x2 60 us: one_after_other(): return lax.psum(partial, other)]
  transfers between devices with their start and end apart: 24 -> 24, of which waited for: 7 -> 7; matrix products, arithmetic and copies ran while one was open for 5% -> 4% of each run, Pallas kernels for 0% -> 0%
where the time goes in v1:
time: 813 us; the launch traced here: 805 us
  blocking collectives  578 us (71%)
  matrix products  70 us (9%)
  starting transfers between devices  67.1 us (8%)
  local copies, waits for them, and re-layouts  57.8 us (7%)
  other arithmetic  24.1 us (3%)
    psum x2, blocking collectives, shards(): alpha = rz_now / lax.psum(inner_local(direction, image), ('rows', 'cols'))  156 us
    unnamed x3, blocking collectives  137 us
    psum x3, blocking collectives, precondition(): owned = lax.psum(owned, 'rows')  90.6 us
    all_gather x3, blocking collectives, precondition(): every_sol = lax.all_gather(own_sol, 'cols', axis=0, tiled=True)  74.4 us
    psum x2, blocking collectives, one_after_other(): return lax.psum(partial, other)  60 us
    psum x2, blocking collectives, one_after_other(): partial = lax.psum(x, one)  59.3 us
    ppermute x12, starting transfers between devices, with_halo(): lax.ppermute(tail, axis, [(i, (i + 1) % count) for i in range(ends)])  46 us
    ppermute x12, starting transfers between devices, with_halo(): lax.ppermute(head, axis, [((i + 1) % count, i) for i in range(ends)])  21.1 us
  transfers between devices with their start and end apart: 24, of which 7 were waited for; matrix products, arithmetic and copies ran while one was open for 4% of the time, Pallas kernels for 0%

profile of v1, /device:TPU:1, one launch (start us, length us, event | category | flops | bytes accessed | tf_op | source)
XLA Modules:
  0.0 805.0 jit_solution(3697912469158105041)
XLA Ops:
  4.4 4.7 collective-permute-start
  12.0 4.0 collective-permute-start.4
  18.6 48.1 %all-reduce.5 = f32[16,16,2]{1,2,0:T(2,128)S(1)} all-reduce(f32[16,16,2]{1,2,0:T(2,128)S(1)} %broadcast_multiply_fusion.3), channel_id=5, replica_groups=mesh['rows'=16,'cols'=16] {'cols'}, use_global_device_ids=true, to_apply=%region_3.4.clone | all-reduce | flops 512 | bytes 4096
  68.0 32.1 %psum.63 = f32[16,2]{0,1:T(2,128)S(1)} all-reduce(f32[16,2]{0,1:T(2,128)S(1)} %dynamic-slice_bitcast_fusion.2), channel_id=1, replica_groups=mesh['rows'=16,'cols'=16] {'rows'}, use_global_device_ids=true, to_apply=%region_4.5 | all-reduce | flops 32 | bytes 256 | tf_op jit(solution)/shard_map/psum | solution.py:151
  100.3 24.5 %all-gather.3 = f32[16,16,2]{1,2,0:T(2,128)S(1)} all-gather(f32[1,16,2]{1,2,0:T(2,128)S(1)} %convolution_bitcast_fusion.8), channel_id=2, replica_groups=mesh['rows'=16,'cols'=16] {'cols'}, dimensions={0}, use_global_device_ids=true | all-gather | bytes 2176 | tf_op jit(solution)/shard_map/all_gather | solution.py:154
  139.4 3.6 collective-permute-start.6
  157.6 3.8 fusion.22
  161.4 4.1 fusion.8
  173.8 4.0 collective-permute-start.8
  185.3 5.0 collective-permute-start.10
  195.4 30.3 %psum.64 = f32[2]{0:T(128)S(1)} all-reduce(f32[2]{0:T(128)S(1)} %get-tuple-element.4), channel_id=1, replica_groups=mesh['rows'=16,'cols'=16] {'rows'}, use_global_device_ids=true, to_apply=%region_6.7 | all-reduce | flops 2 | bytes 16 | tf_op jit(solution)/shard_map/psum | solution.py:17
  225.7 30.0 %psum.65 = f32[2]{0:T(128)S(1)} all-reduce(f32[2]{0:T(128)S(1)} %psum.64), channel_id=1, replica_groups=mesh['rows'=16,'cols'=16] {'cols'}, use_global_device_ids=true, to_apply=%region_7.8 | all-reduce | flops 2 | bytes 16 | tf_op jit(solution)/shard_map/psum | solution.py:18
  255.7 76.4 %psum.66 = f32[2]{0:T(128)S(1)} all-reduce(f32[2]{0:T(128)S(1)} %get-tuple-element.3), channel_id=1, replica_groups=mesh['rows'=16,'cols'=16] {'rows','cols'}, use_global_device_ids=true, to_apply=%region_9.10 | all-reduce | flops 2 | bytes 16 | tf_op jit(solution)/shard_map/psum | solution.py:171
  332.7 45.3 %all-reduce.6 = f32[16,16,2]{1,2,0:T(2,128)S(1)} all-reduce(f32[16,16,2]{1,2,0:T(2,128)S(1)} %broadcast_multiply_fusion.2), channel_id=6, replica_groups=mesh['rows'=16,'cols'=16] {'cols'}, use_global_device_ids=true, to_apply=%region_11.12.clone | all-reduce | flops 512 | bytes 4096
  378.6 29.8 %psum.67 = f32[16,2]{0,1:T(2,128)S(1)} all-reduce(f32[16,2]{0,1:T(2,128)S(1)} %dynamic-slice_bitcast_fusion.1), channel_id=1, replica_groups=mesh['rows'=16,'cols'=16] {'rows'}, use_global_device_ids=true, to_apply=%region_12.13 | all-reduce | flops 32 | bytes 256 | tf_op jit(solution)/shard_map/psum | solution.py:151
  409.8 4.0 collective-permute-start.12
  413.9 25.2 %all-gather.4 = f32[16,16,2]{1,2,0:T(2,128)S(1)} all-gather(f32[1,16,2]{1,2,0:T(2,128)S(1)} %convolution_bitcast_fusion.7), channel_id=3, replica_groups=mesh['rows'=16,'cols'=16] {'cols'}, dimensions={0}, use_global_device_ids=true | all-gather | bytes 2176 | tf_op jit(solution)/shard_map/all_gather | solution.py:154
  467.4 5.2 fusion.16
  476.2 3.8 fusion.20
  480.0 4.1 fusion.4
  487.1 3.9 reshape.324
  493.5 29.0 %psum.68 = f32[2]{0:T(128)S(1)} all-reduce(f32[2]{0:T(128)S(1)} %get-tuple-element.51), channel_id=1, replica_groups=mesh['rows'=16,'cols'=16] {'rows'}, use_global_device_ids=true, to_apply=%region_14.15 | all-reduce | flops 2 | bytes 16 | tf_op jit(solution)/shard_map/psum | solution.py:17
  522.6 30.0 %psum.69 = f32[2]{0:T(128)S(1)} all-reduce(f32[2]{0:T(128)S(1)} %psum.68), channel_id=1, replica_groups=mesh['rows'=16,'cols'=16] {'cols'}, use_global_device_ids=true, to_apply=%region_15.16 | all-reduce | flops 2 | bytes 16 | tf_op jit(solution)/shard_map/psum | solution.py:18
  554.0 4.0 collective-permute-start.16
  574.2 80.1 %psum.70 = f32[2]{0:T(128)S(1)} all-reduce(f32[2]{0:T(128)} %get-tuple-element.15), channel_id=1, replica_groups=mesh['rows'=16,'cols'=16] {'rows','cols'}, use_global_device_ids=true, to_apply=%region_17.18 | all-reduce | flops 2 | bytes 16 | tf_op jit(solution)/shard_map/psum | solution.py:171
  658.0 4.0 collective-permute-start.20
  662.1 43.4 %all-reduce.7 = f32[16,16,2]{1,2,0:T(2,128)S(1)} all-reduce(f32[16,16,2]{1,2,0:T(2,128)S(1)} %broadcast_multiply_fusion.1), channel_id=7, replica_groups=mesh['rows'=16,'cols'=16] {'cols'}, use_global_device_ids=true, to_apply=%region_19.20.clone | all-reduce | flops 512 | bytes 4096
  706.2 28.6 %psum.71 = f32[16,2]{0,1:T(2,128)S(1)} all-reduce(f32[16,2]{0,1:T(2,128)S(1)} %dynamic-slice_bitcast_fusion), channel_id=1, replica_groups=mesh['rows'=16,'cols'=16] {'rows'}, use_global_device_ids=true, to_apply=%region_20.21 | all-reduce | flops 32 | bytes 256 | tf_op jit(solution)/shard_map/psum | solution.py:151
  735.0 24.7 %all-gather.5 = f32[16,16,2]{1,2,0:T(2,128)S(1)} all-gather(f32[1,16,2]{1,2,0:T(2,128)S(1)} %convolution_bitcast_fusion.6), channel_id=4, replica_groups=mesh['rows'=16,'cols'=16] {'cols'}, dimensions={0}, use_global_device_ids=true | all-gather | bytes 2176 | tf_op jit(solution)/shard_map/all_gather | solution.py:154
  782.2 3.7 fusion.14
  789.5 3.8 fusion.18
  793.3 3.9 fusion
  (262 shorter events, 155.8 us)
Async XLA Ops:
  0.6 99.5 %copy-start = (f32[16,16,16]{2,1,0:T(8,128)S(1)}, f32[16,16,16]{2,1,0:T(8,128)}, u32[]{:S(2)}) copy-start(f32[16,16,16]{2,1,0:T(8,128)} %param.11) | copy-start | bytes 49156
  3.1 126.8 %collective-permute-start.1 = (f32[2,4,64,128]{2,3,1,0:T(8,128)}, f32[2,4,64,128]{2,3,1,0:T(8,128)S(1)}, u32[]{:S(2)}, u32[]{:S(2)}) collective-permute-start(f32[2,4,64,128]{2,3,1,0:T(8,128)} %get-tuple-element.43), channel_id=1, source_target_pairs={{16,0},{32,16},{48,32},{64,48},{80,64},{96,80},{112,96},{128,112},... | collective-permute-start | bytes 786440 | tf_op jit(solution)/shard_map/ppermute | solution.py:31
  4.4 125.5 %collective-permute-start = (f32[2,4,64,128]{2,3,1,0:T(8,128)}, f32[2,4,64,128]{2,3,1,0:T(8,128)S(1)}, u32[]{:S(2)}, u32[]{:S(2)}) collective-permute-start(f32[2,4,64,128]{2,3,1,0:T(8,128)} %get-tuple-element.42), channel_id=1, source_target_pairs={{0,16},{16,32},{32,48},{48,64},{64,80},{80,96},{96,112},{112,128},... | collective-permute-start | bytes 786440 | tf_op jit(solution)/shard_map/ppermute | solution.py:29
  9.7 118.2 %copy-start.25 = (f32[4]{0:T(128)}, f32[4]{0:T(128)S(1)}, u32[]{:S(2)}) copy-start(f32[4]{0:T(128)S(1)} %get-tuple-element.5) | copy-start | bytes 52
  9.7 118.2 %copy-start.27 = (f32[4]{0:T(128)}, f32[4]{0:T(128)S(1)}, u32[]{:S(2)}) copy-start(f32[4]{0:T(128)S(1)} %get-tuple-element.6) | copy-start | bytes 52
  9.8 118.2 %copy-start.29 = (f32[4]{0:T(128)}, f32[4]{0:T(128)S(1)}, u32[]{:S(2)}) copy-start(f32[4]{0:T(128)S(1)} %get-tuple-element.7) | copy-start | bytes 52
  9.8 118.2 %copy-start.31 = (f32[4]{0:T(128)}, f32[4]{0:T(128)S(1)}, u32[]{:S(2)}) copy-start(f32[4]{0:T(128)S(1)} %get-tuple-element.8) | copy-start | bytes 52
  9.8 118.2 %copy-start.33 = (f32[4]{0:T(128)}, f32[4]{0:T(128)S(1)}, u32[]{:S(2)}) copy-start(f32[4]{0:T(128)S(1)} %get-tuple-element.9) | copy-start | bytes 52
  9.8 118.2 %copy-start.35 = (f32[4]{0:T(128)}, f32[4]{0:T(128)S(1)}, u32[]{:S(2)}) copy-start(f32[4]{0:T(128)S(1)} %get-tuple-element.10) | copy-start | bytes 52
  10.7 125.5 %collective-permute-start.5 = (f32[1,4,1,128]{3,2,1,0:T(1,128)}, f32[1,4,1,128]{3,2,1,0:T(1,128)S(1)}, u32[]{:S(2)}, u32[]{:S(2)}) collective-permute-start(f32[1,4,1,128]{3,2,1,0:T(1,128)} %get-tuple-element.47), channel_id=1, source_target_pairs={{16,0},{32,16},{48,32},{64,48},{80,64},{96,80},{112,96},{128,112},... | collective-permute-start | bytes 6152 | tf_op jit(solution)/shard_map/ppermute | solution.py:31
  12.0 124.2 %collective-permute-start.4 = (f32[1,4,1,128]{3,2,1,0:T(1,128)}, f32[1,4,1,128]{3,2,1,0:T(1,128)S(1)}, u32[]{:S(2)}, u32[]{:S(2)}) collective-permute-start(f32[1,4,1,128]{3,2,1,0:T(1,128)} %get-tuple-element.46), channel_id=1, source_target_pairs={{0,16},{16,32},{32,48},{48,64},{64,80},{80,96},{96,112},{112,128},... | collective-permute-start | bytes 6152 | tf_op jit(solution)/shard_map/ppermute | solution.py:29
  130.5 17.0 %collective-permute-start.3 = (f32[2,4,256,64]{2,3,1,0:T(8,128)S(1)}, f32[2,4,256,64]{2,3,1,0:T(8,128)S(1)}, u32[]{:S(2)}, u32[]{:S(2)}) collective-permute-start(f32[2,4,256,64]{2,3,1,0:T(8,128)S(1)} %get-tuple-element.25), channel_id=1, source_target_pairs={{1,0},{2,1},{3,2},{4,3},{5,4},{6,5},{7,6},{8,7},{9,8},{10,9},{11,1... | collective-permute-start | bytes 1572872 | tf_op jit(solution)/shard_map/ppermute | solution.py:31
  132.6 14.9 %collective-permute-start.2 = (f32[2,4,256,64]{2,3,1,0:T(8,128)S(1)}, f32[2,4,256,64]{2,3,1,0:T(8,128)S(1)}, u32[]{:S(2)}, u32[]{:S(2)}) collective-permute-start(f32[2,4,256,64]{2,3,1,0:T(8,128)S(1)} %get-tuple-element.24), channel_id=1, source_target_pairs={{0,1},{1,2},{2,3},{3,4},{4,5},{5,6},{6,7},{7,8},{8,9},{9,10},{10,1... | collective-permute-start | bytes 1572872 | tf_op jit(solution)/shard_map/ppermute | solution.py:29
  137.5 7.9 collective-permute-start.7
  139.4 7.1 collective-permute-start.6
  172.5 6.8 collective-permute-start.9
  173.8 5.5 collective-permute-start.8
  182.0 9.1 %collective-permute-start.11 = (f32[2,4,130,1]{2,1,3,0:T(4,128)S(1)}, f32[2,4,130,1]{2,1,3,0:T(4,128)S(1)}, u32[]{:S(2)}, u32[]{:S(2)}) collective-permute-start(f32[2,4,130,1]{2,1,3,0:T(4,128)S(1)} %copy.90), channel_id=1, source_target_pairs={{1,0},{2,1},{3,2},{4,3},{5,4},{6,5},{7,6},{8,7},{9,8},{10,9},{11,1... | collective-permute-start | bytes 12488 | tf_op jit(solution)/shard_map/ppermute | solution.py:31
  185.3 6.8 collective-permute-start.10
  408.5 32.7 %collective-permute-start.13 = (f32[2,4,64,128]{3,2,1,0:T(8,128)S(1)}, f32[2,4,64,128]{3,2,1,0:T(8,128)S(1)}, u32[]{:S(2)}, u32[]{:S(2)}) collective-permute-start(f32[2,4,64,128]{3,2,1,0:T(8,128)S(1)} %get-tuple-element.39), channel_id=1, source_target_pairs={{16,0},{32,16},{48,32},{64,48},{80,64},{96,80},{112,96},{128,112},... | collective-permute-start | bytes 786440 | tf_op jit(solution)/shard_map/ppermute | solution.py:31
  409.8 31.4 %collective-permute-start.12 = (f32[2,4,64,128]{3,2,1,0:T(8,128)S(1)}, f32[2,4,64,128]{3,2,1,0:T(8,128)S(1)}, u32[]{:S(2)}, u32[]{:S(2)}) collective-permute-start(f32[2,4,64,128]{3,2,1,0:T(8,128)S(1)} %get-tuple-element.38), channel_id=1, source_target_pairs={{0,16},{16,32},{32,48},{48,64},{64,80},{80,96},{96,112},{112,128},... | collective-permute-start | bytes 786440 | tf_op jit(solution)/shard_map/ppermute | solution.py:29
  444.9 10.8 %collective-permute-start.15 = (f32[2,4,256,64]{2,3,1,0:T(8,128)}, f32[2,4,256,64]{2,3,1,0:T(8,128)}, u32[]{:S(2)}, u32[]{:S(2)}) collective-permute-start(f32[2,4,256,64]{2,3,1,0:T(8,128)} %copy.97), channel_id=1, source_target_pairs={{1,0},{2,1},{3,2},{4,3},{5,4},{6,5},{7,6},{8,7},{9,8},{10,9},{11,1... | collective-permute-start | bytes 1572872 | tf_op jit(solution)/shard_map/ppermute | solution.py:31
  448.1 9.9 %collective-permute-start.14 = (f32[2,4,256,64]{2,3,1,0:T(8,128)}, f32[2,4,256,64]{2,3,1,0:T(8,128)}, u32[]{:S(2)}, u32[]{:S(2)}) collective-permute-start(f32[2,4,256,64]{2,3,1,0:T(8,128)} %copy.96), channel_id=1, source_target_pairs={{0,1},{1,2},{2,3},{3,4},{4,5},{5,6},{6,7},{7,8},{8,9},{9,10},{10,1... | collective-permute-start | bytes 1572872 | tf_op jit(solution)/shard_map/ppermute | solution.py:29
  552.7 5.3 collective-permute-start.17
  554.0 4.7 collective-permute-start.16
  561.4 7.8 collective-permute-start.19
  566.2 4.1 collective-permute-start.18
  656.7 119.8 %copy-start.2 = (f32[2,4,128,128]{3,2,1,0:T(8,128)}, f32[2,4,128,128]{3,2,1,0:T(8,128)S(1)}, u32[]{:S(2)}) copy-start(f32[2,4,128,128]{3,2,1,0:T(8,128)S(1)} %get-tuple-element.14) | copy-start | bytes 1572868
  656.8 104.1 %collective-permute-start.21 = (f32[2,4,64,128]{3,2,1,0:T(8,128)S(1)}, f32[2,4,64,128]{3,2,1,0:T(8,128)S(1)}, u32[]{:S(2)}, u32[]{:S(2)}) collective-permute-start(f32[2,4,64,128]{3,2,1,0:T(8,128)S(1)} %get-tuple-element.35), channel_id=1, source_target_pairs={{16,0},{32,16},{48,32},{64,48},{80,64},{96,80},{112,96},{128,112},... | collective-permute-start | bytes 786440 | tf_op jit(solution)/shard_map/ppermute | solution.py:31
  658.0 102.8 %collective-permute-start.20 = (f32[2,4,64,128]{3,2,1,0:T(8,128)S(1)}, f32[2,4,64,128]{3,2,1,0:T(8,128)S(1)}, u32[]{:S(2)}, u32[]{:S(2)}) collective-permute-start(f32[2,4,64,128]{3,2,1,0:T(8,128)S(1)} %get-tuple-element.34), channel_id=1, source_target_pairs={{0,16},{16,32},{32,48},{48,64},{64,80},{80,96},{96,112},{112,128},... | collective-permute-start | bytes 786440 | tf_op jit(solution)/shard_map/ppermute | solution.py:29
  763.1 10.7 %collective-permute-start.23 = (f32[2,4,256,64]{2,3,1,0:T(8,128)}, f32[2,4,256,64]{2,3,1,0:T(8,128)S(1)}, u32[]{:S(2)}, u32[]{:S(2)}) collective-permute-start(f32[2,4,256,64]{2,3,1,0:T(8,128)} %copy.115), channel_id=1, source_target_pairs={{1,0},{2,1},{3,2},{4,3},{5,4},{6,5},{7,6},{8,7},{9,8},{10,9},{11,1... | collective-permute-start | bytes 1572872 | tf_op jit(solution)/shard_map/ppermute | solution.py:31
  765.5 9.6 %collective-permute-start.22 = (f32[2,4,256,64]{2,3,1,0:T(8,128)S(1)}, f32[2,4,256,64]{2,3,1,0:T(8,128)}, u32[]{:S(2)}, u32[]{:S(2)}) collective-permute-start(f32[2,4,256,64]{2,3,1,0:T(8,128)S(1)} %copy.114), channel_id=1, source_target_pairs={{0,1},{1,2},{2,3},{3,4},{4,5},{5,6},{6,7},{7,8},{8,9},{9,10},{10,1... | collective-permute-start | bytes 1572872 | tf_op jit(solution)/shard_map/ppermute | solution.py:29
  (45 other events, 576.1 us)
